TPU v7x, 32 devices: a whole 2x2x4 slice. The times are simulated.
32 devices in a mesh: member: 4 (over z), region: 8 (over y, x, core).
Axes of the slice: x: 2, y: 2, z: 4, core: 2. Of those that a mesh axis runs over, the one named last changes fastest.
Arguments:
- background: bfloat16 [64, 13, 192, 1024], P('member', None, 'region'), may hold values from -6 to 6
- obs_ens: bfloat16 [131072, 64], P(('member', 'region')), may hold values from -6 to 6
- obs_value: bfloat16 [131072], P(('member', 'region')), may hold values from -8 to 8
- obs_precision: bfloat16 [131072], P(('member', 'region')), may hold values from 0.0009994507 to 0.0099487305
- obs_row: int32 [131072], P(('member', 'region')), may hold values from 0 to 47
- obs_patch: int32 [131072, 1], P(('member', 'region')), may hold values from 0 to 31; in each aligned block of 4096 rows (0 to 4095, 4096 to 8191, ...) at most 256 rows name the same one
Outputs:
- analysis: bfloat16 [64, 13, 192, 1024], P(None, None, 'member', 'region')
Inputs may be any that keep to these rules, and one draw needn't show every extreme that they name: `obs_patch`: among the observations of one device, at most 256 fall in one patch, and some patch receives exactly 256 of them.
All inputs are finite; a program needn't handle non-finite values.
Results may differ from a plain program's by a relative error of at most 0.0015.
The roundings to bfloat16 on the way count: a program that leaves them out, or rounds other values in their place, can miss the bound.
Values may be sent and summed in bfloat16 or wider, within the bound.
A program may use at most 128 MiB of HBM per device.

v0:
```python
import math

import jax
import jax.numpy as jnp
from jax import lax
from jax.sharding import PartitionSpec as P

BAND = 2
NS_ITERS = 4


def batched(left, right):
    return jnp.einsum("bij,bjk->bik", left, right, precision=lax.Precision.HIGHEST)


def localize(row_float, obs_prec, lat_rows):
    centers = jnp.arange(lat_rows // BAND, dtype=jnp.float32) * BAND + (BAND - 1) / 2.0
    distance = (row_float[None, :] - centers[:, None]) / (lat_rows / 4.0)
    return obs_prec[None, :] * jnp.exp(-0.5 * distance * distance)


def band_transforms(ens_vals, obs_val, obs_prec, row_float, lat_rows):
    members = ens_vals.shape[1]
    ens_float = ens_vals.astype(jnp.float32)
    ens_mean = jnp.sum(ens_float, axis=1) / members
    ens_pert = (ens_float - ens_mean[:, None]).astype(jnp.bfloat16)
    pert_float = ens_pert.astype(jnp.float32)
    innovation = obs_val - ens_mean
    weight = localize(row_float, obs_prec, lat_rows)

    def band_gram(band_weight):
        scaled = (band_weight[:, None] * pert_float).astype(jnp.bfloat16)
        return lax.dot_general(
            scaled, ens_pert, (((0,), (0,)), ((), ())), preferred_element_type=jnp.float32
        )

    gram_band = lax.map(band_gram, weight)
    projected = jnp.dot(weight * innovation[None, :], pert_float, precision=lax.Precision.HIGHEST)
    identity = jnp.eye(members, dtype=jnp.float32)
    system = (members - 1.0) * identity + gram_band
    norm_f = jnp.sqrt(jnp.sum(system * system, axis=(1, 2)))
    root_iter = system / norm_f[:, None, None]
    inv_root = jnp.broadcast_to(identity, system.shape)
    for newton_step in range(NS_ITERS):
        middle = 1.5 * identity - 0.5 * batched(inv_root, root_iter)
        root_iter = batched(root_iter, middle)
        inv_root = batched(middle, inv_root)
    spread = jnp.sqrt((members - 1.0) / norm_f)[:, None, None] * inv_root
    inverse = batched(inv_root, inv_root) / norm_f[:, None, None]
    mean_shift = jnp.einsum("bjk,bk->bj", inverse, projected, precision=lax.Precision.HIGHEST)
    return (spread + mean_shift[:, :, None]).astype(jnp.bfloat16)


def slot_numbers(target_patch, devices, capacity):
    obs_rows = target_patch.shape[0]
    block = math.gcd(obs_rows, 512)
    nblock = obs_rows // block
    onehot = (target_patch[:, None] == jnp.arange(devices, dtype=jnp.int32)[None, :]).astype(
        jnp.bfloat16
    )
    blocks = onehot.reshape(nblock, block, devices)
    lower = (jnp.arange(block)[:, None] > jnp.arange(block)[None, :]).astype(jnp.bfloat16)
    inner = jnp.einsum("ij,bjd->bid", lower, blocks, preferred_element_type=jnp.float32)
    totals = jnp.sum(blocks, axis=1, dtype=jnp.float32)
    offsets = jnp.cumsum(totals, axis=0) - totals
    before = inner + offsets[:, None, :]
    rank = jnp.sum(before * blocks.astype(jnp.float32), axis=2).reshape(obs_rows).astype(jnp.int32)
    return target_patch * capacity + rank


def local(background, obs_ens, obs_value, obs_precision, obs_row, obs_patch):
    members = lax.axis_size("member")
    regions = lax.axis_size("region")
    devices = members * regions
    obs_rows = obs_row.shape[0]
    capacity = 2 * obs_rows // devices
    total_slots = devices * capacity
    width = obs_ens.shape[1]
    target_patch = obs_patch[:, 0]
    slots = slot_numbers(target_patch, devices, capacity)
    packed_cols = (width + 3 + 127) // 128 * 128
    extras = jnp.stack([obs_value, obs_precision, obs_row.astype(jnp.bfloat16)], axis=1)
    filler = jnp.zeros((obs_rows, packed_cols - width - 3), jnp.bfloat16)
    packed = jnp.concatenate([obs_ens, extras, filler], axis=1)
    slot_block = math.gcd(total_slots, 512)

    def fill_block(start):
        wanted = start + jnp.arange(slot_block, dtype=jnp.int32)
        select = (wanted[:, None] == slots[None, :]).astype(jnp.bfloat16)
        return jnp.dot(select, packed, preferred_element_type=jnp.float32).astype(jnp.bfloat16)

    buffer = lax.map(
        fill_block, jnp.arange(total_slots // slot_block, dtype=jnp.int32) * slot_block
    )
    buffer = buffer.reshape(total_slots, packed_cols)
    ens_buf = buffer[:, :width]
    value_buf = buffer[:, width]
    prec_buf = buffer[:, width + 1]
    row_buf = buffer[:, width + 2]
    ens_recv, value_recv, prec_recv, row_recv = (
        lax.all_to_all(ens_buf, ("member", "region"), split_axis=0, concat_axis=0, tiled=True),
        lax.all_to_all(value_buf, ("member", "region"), split_axis=0, concat_axis=0, tiled=True),
        lax.all_to_all(prec_buf, ("member", "region"), split_axis=0, concat_axis=0, tiled=True),
        lax.all_to_all(row_buf, ("member", "region"), split_axis=0, concat_axis=0, tiled=True),
    )
    local_members = background.shape[0]
    channels = background.shape[1]
    rows_local = background.shape[2]
    lon_cols = background.shape[3] // regions
    strips_each = regions // members
    lat_rows = strips_each * rows_local
    prepared = background.reshape(local_members, channels, rows_local, regions, lon_cols).transpose(
        3, 0, 1, 2, 4
    )
    arrived = lax.all_to_all(
        lax.all_to_all(prepared, "region", split_axis=0, concat_axis=0, tiled=True),
        "member",
        split_axis=0,
        concat_axis=0,
        tiled=True,
    )
    patch_states = arrived.reshape(
        members, strips_each, local_members, channels, rows_local, lon_cols
    )
    member_axes = (0, 2)
    layout = "mrjcxl"
    transform = band_transforms(
        ens_recv,
        value_recv.astype(jnp.float32),
        prec_recv.astype(jnp.float32),
        row_recv.astype(jnp.float32),
        lat_rows,
    )
    state_mean = jnp.sum(patch_states, axis=member_axes, dtype=jnp.float32) / width
    state_pert = (
        patch_states.astype(jnp.float32) - jnp.expand_dims(state_mean, member_axes)
    ).astype(jnp.bfloat16)
    row_transform = jnp.repeat(transform, BAND, axis=0).reshape(
        strips_each, rows_local, members, local_members, width
    )
    increment = jnp.einsum(
        layout + ",rxmjk->kcrxl", state_pert, row_transform, preferred_element_type=jnp.float32
    )
    result = state_mean.transpose(1, 0, 2, 3)[None] + increment
    return result.reshape(width, channels, lat_rows, lon_cols).astype(jnp.bfloat16)


def solution(mesh):
    in_specs = (
        P("member", None, "region", None),
        P(("member", "region"), None),
        P(("member", "region")),
        P(("member", "region")),
        P(("member", "region")),
        P(("member", "region"), None),
    )
    out_specs = P(None, None, "member", "region")
    return jax.shard_map(local, mesh=mesh, in_specs=in_specs, out_specs=out_specs, check_vma=False)
```

profile of v0, /device:TPU:2, one launch (start us, length us, event | category | flops | bytes accessed | tf_op | source)
XLA Modules:
  0.0 534.4 jit_solution(3356309672877438282)
XLA Ops:
  10.6 6.4 %concatenate.3 = bf16[4096,128]{1,0:T(8,128)(2,1)} concatenate(bf16[4096,64]{1,0:T(8,128)(2,1)} %copy.68, bf16[4096,1]{1,0:T(8,128)(2,1)} %stack.12, bf16[4096,1]{1,0:T(8,128)(2,1)} %stack.13, bf16[4096,1]{1,0:T(8,128)(2,1)S(1)} %stack.14, bf16[4096,61]{1,0:T(8,128)(2,1)} %broadcast_in_dim.25), dimensions={1} | concatenate | bytes 2097152 | tf_op jit(solution)/shard_map/concatenate | solution.py:84
  17.0 61.4 %while.20 = (s32[]{:T(128)}, bf16[16,512,128]{2,1,0:T(8,128)(2,1)S(1)}, s32[16]{0:T(128)S(1)}, s32[4096]{0:T(1024)S(1)}, bf16[4096,128]{1,0:T(8,128)(2,1)}, /*index=5*/s32[]{:T(128)}) while((s32[]{:T(128)}, bf16[16,512,128]{2,1,0:T(8,128)(2,1)S(1)}, s32[16]{0:T(128)S(1)}, s32[4096]{0:T(1024)S(1)}, bf16[4096,128]{1,0:T(8,128)(2,1)}, ...), condition=%wide.region_6.7_spmd, body=%wide.region_5.6_spmd.sunk | while | flops 539034112 | bytes 1200225 | solution.py:92
  86.6 6.1 %all-to-all-start.5 = ((bf16[32,2,128]{2,1,0:T(2,128)(2,1)}), bf16[32,2,128]{2,1,0:T(2,128)(2,1)S(1)}, u32[]{:S(2)}, u32[]{:S(2)}) async-start(bf16[32,2,128]{2,1,0:T(2,128)(2,1)} %reshape.155), calls=%async_computation.5 | async-start | bytes 32768 | tf_op jit(solution)/shard_map/all_to_all | solution.py:102
  122.3 10.5 %copy.99 = bf16[624,8,8,128]{3,2,1,0:T(8,128)(2,1)} copy(bf16[624,8,8,128]{3,1,2,0:T(8,128)(2,1)} %bitcast.123) | data formatting | bytes 20447232
  132.8 9.0 %copy.65 = bf16[8,16,13,24,128]{4,3,2,1,0:T(8,128)(2,1)} copy(bf16[8,16,13,24,128]{4,0,3,2,1:T(8,128)(2,1)} %bitcast.120) | data formatting | bytes 20447232 | tf_op jit(solution)/shard_map/transpose | solution.py:112
  141.9 6.3 %all-to-all-done.4 = bf16[32,256,64]{1,2,0:T(8,128)(2,1)S(1)} async-done(((bf16[32,256,64]{1,2,0:T(8,128)(2,1)}), bf16[32,256,64]{1,2,0:T(8,128)(2,1)S(1)}, u32[]{:S(2)}, u32[]{:S(2)}) %all-to-all-start.4) | async-done | bytes 1048608 | tf_op jit(solution)/shard_map/all_to_all | solution.py:101
  159.5 106.6 %all-to-all-done = bf16[8,16,13,24,128]{4,3,2,1,0:T(8,128)(2,1)} async-done(((bf16[8,16,13,24,128]{4,3,2,1,0:T(8,128)(2,1)}), bf16[8,16,13,24,128]{4,3,2,1,0:T(8,128)(2,1)}, u32[]{:S(2)}, u32[]{:S(2)}) %all-to-all-start) | async-done | bytes 10223648 | tf_op jit(solution)/shard_map/all_to_all | solution.py:116
  272.0 169.7 %while.21 = (s32[]{:T(128)}, f32[24,64,64]{2,1,0:T(8,128)}, f32[24,8192]{1,0:T(8,128)}, f32[8192,64]{1,0:T(8,128)}, bf16[8192,64]{1,0:T(8,128)(2,1)S(1)}, /*index=5*/s32[]{:T(128)}) while((s32[]{:T(128)}, f32[24,64,64]{2,1,0:T(8,128)}, f32[24,8192]{1,0:T(8,128)}, f32[8192,64]{1,0:T(8,128)}, bf16[8192,64]{1,0:T(8,128)(2,1)S(1)}, ...), condition=%wide.region_9.10_spmd, body=%wide.region_8.9_spmd.sunk | while | flops 68157440 | bytes 5374037 | solution.py:37
  280.0 6.1 %fusion.92 = f32[24,64,64]{2,1,0:T(8,128)} fusion(f32[24,64,64]{2,1,0:T(8,128)} %get-tuple-element.187, s32[]{:T(128)S(6)} %copy.119, bf16[8192,64]{1,0:T(8,128)(2,1)S(1)} %get-tuple-element.196, f32[8192,64]{1,0:T(8,128)} %get-tuple-element.195, f32[8192]{0:T(1024)S(1)} %bitcast.126), kind=kOutput, calls=%fused_computation.12.clone.1 | convolution fusion | flops 68157440 | bytes 5308420 | tf_op jit(solution)/shard_map/while/body/eval_jaxpr/dot_general | solution.py:33
  294.1 6.1 %fusion.92 = f32[24,64,64]{2,1,0:T(8,128)} fusion(f32[24,64,64]{2,1,0:T(8,128)} %get-tuple-element.187, s32[]{:T(128)S(6)} %copy.119, bf16[8192,64]{1,0:T(8,128)(2,1)S(1)} %get-tuple-element.196, f32[8192,64]{1,0:T(8,128)} %get-tuple-element.195, f32[8192]{0:T(1024)S(1)} %bitcast.126), kind=kOutput, calls=%fused_computation.12.clone.1 | convolution fusion | flops 68157440 | bytes 5308420 | tf_op jit(solution)/shard_map/while/body/eval_jaxpr/dot_general | solution.py:33
  301.2 6.1 %fusion.92 = f32[24,64,64]{2,1,0:T(8,128)} fusion(f32[24,64,64]{2,1,0:T(8,128)} %get-tuple-element.187, s32[]{:T(128)S(6)} %copy.119, bf16[8192,64]{1,0:T(8,128)(2,1)S(1)} %get-tuple-element.196, f32[8192,64]{1,0:T(8,128)} %get-tuple-element.195, f32[8192]{0:T(1024)S(1)} %bitcast.126), kind=kOutput, calls=%fused_computation.12.clone.1 | convolution fusion | flops 68157440 | bytes 5308420 | tf_op jit(solution)/shard_map/while/body/eval_jaxpr/dot_general | solution.py:33
  308.2 6.1 %fusion.92 = f32[24,64,64]{2,1,0:T(8,128)} fusion(f32[24,64,64]{2,1,0:T(8,128)} %get-tuple-element.187, s32[]{:T(128)S(6)} %copy.119, bf16[8192,64]{1,0:T(8,128)(2,1)S(1)} %get-tuple-element.196, f32[8192,64]{1,0:T(8,128)} %get-tuple-element.195, f32[8192]{0:T(1024)S(1)} %bitcast.126), kind=kOutput, calls=%fused_computation.12.clone.1 | convolution fusion | flops 68157440 | bytes 5308420 | tf_op jit(solution)/shard_map/while/body/eval_jaxpr/dot_general | solution.py:33
  322.3 6.1 %fusion.92 = f32[24,64,64]{2,1,0:T(8,128)} fusion(f32[24,64,64]{2,1,0:T(8,128)} %get-tuple-element.187, s32[]{:T(128)S(6)} %copy.119, bf16[8192,64]{1,0:T(8,128)(2,1)S(1)} %get-tuple-element.196, f32[8192,64]{1,0:T(8,128)} %get-tuple-element.195, f32[8192]{0:T(1024)S(1)} %bitcast.126), kind=kOutput, calls=%fused_computation.12.clone.1 | convolution fusion | flops 68157440 | bytes 5308420 | tf_op jit(solution)/shard_map/while/body/eval_jaxpr/dot_general | solution.py:33
  350.5 6.1 %fusion.92 = f32[24,64,64]{2,1,0:T(8,128)} fusion(f32[24,64,64]{2,1,0:T(8,128)} %get-tuple-element.187, s32[]{:T(128)S(6)} %copy.119, bf16[8192,64]{1,0:T(8,128)(2,1)S(1)} %get-tuple-element.196, f32[8192,64]{1,0:T(8,128)} %get-tuple-element.195, f32[8192]{0:T(1024)S(1)} %bitcast.126), kind=kOutput, calls=%fused_computation.12.clone.1 | convolution fusion | flops 68157440 | bytes 5308420 | tf_op jit(solution)/shard_map/while/body/eval_jaxpr/dot_general | solution.py:33
  364.6 6.1 %fusion.92 = f32[24,64,64]{2,1,0:T(8,128)} fusion(f32[24,64,64]{2,1,0:T(8,128)} %get-tuple-element.187, s32[]{:T(128)S(6)} %copy.119, bf16[8192,64]{1,0:T(8,128)(2,1)S(1)} %get-tuple-element.196, f32[8192,64]{1,0:T(8,128)} %get-tuple-element.195, f32[8192]{0:T(1024)S(1)} %bitcast.126), kind=kOutput, calls=%fused_computation.12.clone.1 | convolution fusion | flops 68157440 | bytes 5308420 | tf_op jit(solution)/shard_map/while/body/eval_jaxpr/dot_general | solution.py:33
  378.7 6.1 %fusion.92 = f32[24,64,64]{2,1,0:T(8,128)} fusion(f32[24,64,64]{2,1,0:T(8,128)} %get-tuple-element.187, s32[]{:T(128)S(6)} %copy.119, bf16[8192,64]{1,0:T(8,128)(2,1)S(1)} %get-tuple-element.196, f32[8192,64]{1,0:T(8,128)} %get-tuple-element.195, f32[8192]{0:T(1024)S(1)} %bitcast.126), kind=kOutput, calls=%fused_computation.12.clone.1 | convolution fusion | flops 68157440 | bytes 5308420 | tf_op jit(solution)/shard_map/while/body/eval_jaxpr/dot_general | solution.py:33
  392.8 6.1 %fusion.92 = f32[24,64,64]{2,1,0:T(8,128)} fusion(f32[24,64,64]{2,1,0:T(8,128)} %get-tuple-element.187, s32[]{:T(128)S(6)} %copy.119, bf16[8192,64]{1,0:T(8,128)(2,1)S(1)} %get-tuple-element.196, f32[8192,64]{1,0:T(8,128)} %get-tuple-element.195, f32[8192]{0:T(1024)S(1)} %bitcast.126), kind=kOutput, calls=%fused_computation.12.clone.1 | convolution fusion | flops 68157440 | bytes 5308420 | tf_op jit(solution)/shard_map/while/body/eval_jaxpr/dot_general | solution.py:33
  399.8 6.1 %fusion.92 = f32[24,64,64]{2,1,0:T(8,128)} fusion(f32[24,64,64]{2,1,0:T(8,128)} %get-tuple-element.187, s32[]{:T(128)S(6)} %copy.119, bf16[8192,64]{1,0:T(8,128)(2,1)S(1)} %get-tuple-element.196, f32[8192,64]{1,0:T(8,128)} %get-tuple-element.195, f32[8192]{0:T(1024)S(1)} %bitcast.126), kind=kOutput, calls=%fused_computation.12.clone.1 | convolution fusion | flops 68157440 | bytes 5308420 | tf_op jit(solution)/shard_map/while/body/eval_jaxpr/dot_general | solution.py:33
  406.9 6.1 %fusion.92 = f32[24,64,64]{2,1,0:T(8,128)} fusion(f32[24,64,64]{2,1,0:T(8,128)} %get-tuple-element.187, s32[]{:T(128)S(6)} %copy.119, bf16[8192,64]{1,0:T(8,128)(2,1)S(1)} %get-tuple-element.196, f32[8192,64]{1,0:T(8,128)} %get-tuple-element.195, f32[8192]{0:T(1024)S(1)} %bitcast.126), kind=kOutput, calls=%fused_computation.12.clone.1 | convolution fusion | flops 68157440 | bytes 5308420 | tf_op jit(solution)/shard_map/while/body/eval_jaxpr/dot_general | solution.py:33
  428.0 6.1 %fusion.92 = f32[24,64,64]{2,1,0:T(8,128)} fusion(f32[24,64,64]{2,1,0:T(8,128)} %get-tuple-element.187, s32[]{:T(128)S(6)} %copy.119, bf16[8192,64]{1,0:T(8,128)(2,1)S(1)} %get-tuple-element.196, f32[8192,64]{1,0:T(8,128)} %get-tuple-element.195, f32[8192]{0:T(1024)S(1)} %bitcast.126), kind=kOutput, calls=%fused_computation.12.clone.1 | convolution fusion | flops 68157440 | bytes 5308420 | tf_op jit(solution)/shard_map/while/body/eval_jaxpr/dot_general | solution.py:33
  457.1 37.8 %all-to-all-done.1 = bf16[8,16,13,24,128]{4,3,2,1,0:T(8,128)(2,1)} async-done(((bf16[8,16,13,24,128]{4,3,2,1,0:T(8,128)(2,1)}), bf16[8,16,13,24,128]{4,3,2,1,0:T(8,128)(2,1)}, u32[]{:S(2)}, u32[]{:S(2)}) %all-to-all-start.1) | async-done | bytes 10223648 | tf_op jit(solution)/shard_map/all_to_all | solution.py:115
  500.6 9.9 %subtract_convert_fusion = bf16[4,2,16,13,24,128]{5,4,3,2,1,0:T(8,128)(2,1)} fusion(f32[2,13,24,128]{3,2,1,0:T(8,128)S(1)} %broadcast_multiply_fusion, bf16[4,2,16,13,24,128]{5,4,3,2,1,0:T(8,128)(2,1)} %bitcast.68), kind=kLoop, calls=%fused_computation.16 | loop fusion | flops 15335424 | bytes 20766720 | tf_op jit(solution)/shard_map/convert_element_type | solution.py:137
  510.8 9.0 %fusion.17 = bf16[64,13,2,24,128]{4,0,1,3,2:T(8,128)(2,1)} fusion(f32[13,2,24,128]{3,0,2,1:T(8,128)S(1)} %copy.67, bf16[2,24,4,16,64,1]{4,3,2,5,1,0:T(8,128)(2,1)S(1)} %bitcast.127, bf16[4,2,16,13,24,128]{5,4,3,2,1,0:T(8,128)(2,1)} %subtract_convert_fusion), kind=kOutput, calls=%fused_computation.15 | convolution fusion | flops 664535040 | bytes 21159936 | tf_op jit(solution)/shard_map/mrjcxl,rxmjk->kcrxl/dot_general | solution.py:141
  519.7 14.5 %copy.85 = bf16[64,13,48,128]{3,2,1,0:T(8,128)(2,1)} copy(bf16[64,13,48,128]{3,0,1,2:T(8,128)(2,1)} %bitcast.119) | data formatting | bytes 20447232 | tf_op jit(solution)/shard_map/convert_element_type | solution.py:145
  (171 shorter events, 243.8 us)
Async XLA Ops:
  0.0 6.2 %copy-start.1 = (bf16[4096]{0:T(1024)(128)(2,1)S(1)}, bf16[4096]{0:T(1024)(128)(2,1)}, u32[]{:S(2)}) copy-start(bf16[4096]{0:T(1024)(128)(2,1)} %param.12) | copy-start | bytes 24580
  3.2 4.7 copy-start.2
  86.6 12.1 %all-to-all-start.5 = ((bf16[32,2,128]{2,1,0:T(2,128)(2,1)}), bf16[32,2,128]{2,1,0:T(2,128)(2,1)S(1)}, u32[]{:S(2)}, u32[]{:S(2)}) async-start(bf16[32,2,128]{2,1,0:T(2,128)(2,1)} %reshape.155), calls=%async_computation.5 | async-start | bytes 32768 | tf_op jit(solution)/shard_map/all_to_all | solution.py:102
  98.7 9.7 %all-to-all-start.3 = ((bf16[32,2,128]{2,1,0:T(2,128)(2,1)}), bf16[32,2,128]{2,1,0:T(2,128)(2,1)S(1)}, u32[]{:S(2)}, u32[]{:S(2)}) async-start(bf16[32,2,128]{2,1,0:T(2,128)(2,1)} %reshape.151), calls=%async_computation.3 | async-start | bytes 32768 | tf_op jit(solution)/shard_map/all_to_all | solution.py:104
  108.4 9.7 %all-to-all-start.2 = ((bf16[32,2,128]{2,1,0:T(2,128)(2,1)}), bf16[32,2,128]{2,1,0:T(2,128)(2,1)S(1)}, u32[]{:S(2)}, u32[]{:S(2)}) async-start(bf16[32,2,128]{2,1,0:T(2,128)(2,1)} %reshape.153), calls=%async_computation.2 | async-start | bytes 32768 | tf_op jit(solution)/shard_map/all_to_all | solution.py:103
  118.1 30.1 %all-to-all-start.4 = ((bf16[32,256,64]{1,2,0:T(8,128)(2,1)}), bf16[32,256,64]{1,2,0:T(8,128)(2,1)S(1)}, u32[]{:S(2)}, u32[]{:S(2)}) async-start(bf16[32,256,64]{1,2,0:T(8,128)(2,1)} %copy.77), calls=%async_computation.4 | async-start | bytes 2097152 | tf_op jit(solution)/shard_map/all_to_all | solution.py:101
  148.2 117.8 %all-to-all-start = ((bf16[8,16,13,24,128]{4,3,2,1,0:T(8,128)(2,1)}), bf16[8,16,13,24,128]{4,3,2,1,0:T(8,128)(2,1)}, u32[]{:S(2)}, u32[]{:S(2)}) async-start(bf16[8,16,13,24,128]{4,3,2,1,0:T(8,128)(2,1)} %copy.65), calls=%async_computation | async-start | bytes 20447232 | tf_op jit(solution)/shard_map/all_to_all | solution.py:116
  266.0 228.8 %all-to-all-start.1 = ((bf16[8,16,13,24,128]{4,3,2,1,0:T(8,128)(2,1)}), bf16[8,16,13,24,128]{4,3,2,1,0:T(8,128)(2,1)}, u32[]{:S(2)}, u32[]{:S(2)}) async-start(bf16[8,16,13,24,128]{4,3,2,1,0:T(8,128)(2,1)} %all-to-all-done), calls=%async_computation.1 | async-start | bytes 20447232 | tf_op jit(solution)/shard_map/all_to_all | solution.py:115
  441.6 2.6 copy-start
where the time goes:
time: 544 us; the launch traced here: 534 us
  matrix products  210 us (39%)
  waiting for transfers between devices  160 us (29%)
  local copies, waits for them, and re-layouts  99.7 us (18%)
  other arithmetic  33.8 us (6%)
  starting transfers between devices  29 us (5%)
    dot_general x24, matrix products, band_gram(): lax.dot_general(scaled, ens_pert, (((0,), (0,)), ((), ())), preferred_ele...  146 us
    all_to_all x1, waiting for transfers between devices, local(): lax.all_to_all(prepared, 'region', split_axis=0, concat_axis=0, tiled=True)  107 us
    dot_general x16, matrix products, fill_block(): jnp.dot(select, packed, preferred_element_type=jnp.float32)  41.3 us
    all_to_all x1, waiting for transfers between devices, local(): lax.all_to_all(lax.all_to_all(prepared, 'region', split_axis=0, concat_ax...  37.8 us
    dynamic_slice x24, local copies, waits for them, and re-layouts, band_transforms(): gram_band = lax.map(band_gram, weight)  23.4 us
    unnamed x22, local copies, waits for them, and re-layouts  22 us
    convert_element_type x1, local copies, waits for them, and re-layouts, local(): result.reshape(width, channels, lat_rows, lon_cols).astype(jnp.bfloat16)  14.5 us
    dot_general x12, matrix products, batched(): jnp.einsum('bij,bjk->bik', left, right, precision=lax.Precision.HIGHEST)  11.1 us
  transfers between devices with their start and end apart: 6, of which 6 were waited for; matrix products, arithmetic and copies ran while one was open for 41% of the time, Pallas kernels for 0%

commit v1 on v0

v1 whole, which is shorter than its diff:
```python
import functools
import math

import jax
import jax.numpy as jnp
from jax import lax
from jax.experimental import pallas as pl
from jax.experimental.pallas import tpu as pltpu
from jax.sharding import PartitionSpec as P


BAND = 2
NS_ITERS = 4
PIECES = 4


def batched(left, right):
    return jnp.einsum("bij,bjk->bik", left, right, precision=lax.Precision.HIGHEST)


def gram_kernel(width, lat_rows, recv_ref, gram_ref, proj_ref, scaled_ref):
    bands = lat_rows // BAND

    @pl.when(pl.program_id(0) == 0)
    def _():
        gram_ref[...] = jnp.zeros_like(gram_ref)
        proj_ref[...] = jnp.zeros_like(proj_ref)

    cols = recv_ref[...].astype(jnp.float32).T
    ens = cols[:width]
    obs_val, obs_prec, row = (cols[width + k : width + k + 1] for k in range(3))
    mean = jnp.sum(ens, axis=0, keepdims=True) / width
    pert = (ens - mean).astype(jnp.bfloat16)
    pert_float = pert.astype(jnp.float32)
    innovation = obs_val - mean
    index = lax.broadcasted_iota(jnp.int32, (bands, 1), 0).astype(jnp.float32)
    distance = (row - (index * BAND + (BAND - 1) / 2.0)) / (lat_rows / 4.0)
    weight = obs_prec * jnp.exp(-0.5 * distance * distance)
    for j in range(bands):
        scaled_ref[j * width : (j + 1) * width, :] = (weight[j : j + 1] * pert_float).astype(
            jnp.bfloat16
        )
    over_obs = (((1,), (1,)), ((), ()))
    gram_ref[...] += lax.dot_general(
        scaled_ref[...], pert, over_obs, preferred_element_type=jnp.float32
    )
    proj_ref[...] += lax.dot_general(
        weight * innovation,
        pert_float,
        over_obs,
        precision=lax.Precision.HIGHEST,
        preferred_element_type=jnp.float32,
    )


def band_grams(recv, width, lat_rows):
    slots, cols = recv.shape
    bands = lat_rows // BAND
    block = math.gcd(slots, 1024)
    gram, projected = pl.pallas_call(
        functools.partial(gram_kernel, width, lat_rows),
        grid=(slots // block,),
        in_specs=[pl.BlockSpec((block, cols), lambda i: (i, 0))],
        out_specs=[
            pl.BlockSpec((bands * width, width), lambda i: (0, 0)),
            pl.BlockSpec((bands, width), lambda i: (0, 0)),
        ],
        out_shape=[
            jax.ShapeDtypeStruct((bands * width, width), jnp.float32),
            jax.ShapeDtypeStruct((bands, width), jnp.float32),
        ],
        scratch_shapes=[pltpu.VMEM((bands * width, block), jnp.bfloat16)],
        compiler_params=pltpu.CompilerParams(vmem_limit_bytes=24 << 20),
        cost_estimate=pl.CostEstimate(
            flops=8 * slots * bands * width * width,
            bytes_accessed=2 * slots * cols,
            transcendentals=slots * bands,
        ),
    )(recv)
    return gram.reshape(bands, width, width), projected


def batched(left, right):
    return jnp.einsum("bij,bjk->bik", left, right, precision=lax.Precision.HIGHEST)


def band_transforms(grams, members):
    gram_band, projected = grams
    identity = jnp.eye(members, dtype=jnp.float32)
    system = (members - 1.0) * identity + gram_band
    norm_f = jnp.sqrt(jnp.sum(system * system, axis=(1, 2)))
    root_iter = system / norm_f[:, None, None]
    inv_root = jnp.broadcast_to(identity, system.shape)
    for _ in range(NS_ITERS):
        middle = 1.5 * identity - 0.5 * batched(inv_root, root_iter)
        root_iter = batched(root_iter, middle)
        inv_root = batched(middle, inv_root)
    spread = jnp.sqrt((members - 1.0) / norm_f)[:, None, None] * inv_root
    inverse = batched(inv_root, inv_root) / norm_f[:, None, None]
    mean_shift = jnp.einsum("bjk,bk->bj", inverse, projected, precision=lax.Precision.HIGHEST)
    return (spread + mean_shift[:, :, None]).astype(jnp.bfloat16)


def slot_numbers(target_patch, devices, capacity):
    obs_rows = target_patch.shape[0]
    block = math.gcd(obs_rows, 512)
    nblock = obs_rows // block
    onehot = (target_patch[:, None] == jnp.arange(devices, dtype=jnp.int32)[None, :]).astype(
        jnp.bfloat16
    )
    blocks = onehot.reshape(nblock, block, devices)
    lower = (jnp.arange(block)[:, None] > jnp.arange(block)[None, :]).astype(jnp.bfloat16)
    inner = jnp.einsum("ij,bjd->bid", lower, blocks, preferred_element_type=jnp.float32)
    totals = jnp.sum(blocks, axis=1, dtype=jnp.float32)
    offsets = jnp.cumsum(totals, axis=0) - totals
    before = inner + offsets[:, None, :]
    rank = jnp.sum(before * blocks.astype(jnp.float32), axis=2).reshape(obs_rows).astype(jnp.int32)
    return target_patch * capacity + rank


def dispatch_kernel(slots_ref, packed_ref, out_ref, wide_ref):
    obs_rows = packed_ref.shape[0]
    wide_ref[...] = jnp.zeros_like(wide_ref)
    unroll = math.gcd(obs_rows, 16)

    def place(step, carry):
        for k in range(unroll):
            i = step * unroll + k
            wide_ref[pl.ds(slots_ref[i], 1), :] = packed_ref[pl.ds(i, 1), :]
        return carry

    lax.fori_loop(0, obs_rows // unroll, place, 0)
    out_ref[...] = wide_ref[...].astype(jnp.bfloat16)


def dispatch(slots, packed, total_slots):
    obs_rows, cols = packed.shape
    return pl.pallas_call(
        dispatch_kernel,
        in_specs=[
            pl.BlockSpec(memory_space=pltpu.SMEM),
            pl.BlockSpec(memory_space=pltpu.VMEM),
        ],
        out_specs=pl.BlockSpec(memory_space=pltpu.VMEM),
        out_shape=jax.ShapeDtypeStruct((total_slots, cols), jnp.bfloat16),
        scratch_shapes=[pltpu.VMEM((total_slots, cols), jnp.float32)],
        compiler_params=pltpu.CompilerParams(vmem_limit_bytes=24 << 20),
        cost_estimate=pl.CostEstimate(
            flops=1 << 32, bytes_accessed=8 * obs_rows * cols, transcendentals=0
        ),
    )(slots, packed)


def scatter_step(spread, shift, strips_each):
    members = lax.axis_size("member")
    target = lax.rem(lax.axis_index("member") + shift, members)
    block = lax.dynamic_slice_in_dim(spread, target * strips_each, strips_each, axis=0)
    if shift == 0:
        return block
    ring = [(k, (k + shift) % members) for k in range(members)]
    return lax.ppermute(block, "member", ring)


def local(background, obs_ens, obs_value, obs_precision, obs_row, obs_patch):
    members = lax.axis_size("member")
    regions = lax.axis_size("region")
    devices = members * regions
    obs_rows = obs_row.shape[0]
    capacity = 2 * obs_rows // devices
    total_slots = devices * capacity
    width = obs_ens.shape[1]
    target_patch = obs_patch[:, 0]
    slots = slot_numbers(target_patch, devices, capacity)
    packed_cols = (width + 3 + 127) // 128 * 128
    extras = jnp.stack([obs_value, obs_precision, obs_row.astype(jnp.bfloat16)], axis=1)
    filler = jnp.zeros((obs_rows, packed_cols - width - 3), jnp.bfloat16)
    packed = jnp.concatenate([obs_ens, extras, filler], axis=1)
    buffer = dispatch(slots, packed.astype(jnp.float32), total_slots)
    local_members = background.shape[0]
    channels = background.shape[1]
    rows_local = background.shape[2]
    lon_cols = background.shape[3] // regions
    strips_each = regions // members
    lat_rows = strips_each * rows_local
    edges = [channels * k // PIECES for k in range(PIECES + 1)]

    def analyse(piece, row_transform):
        patch_states = jnp.stack(piece)
        state_mean = jnp.sum(patch_states, axis=(0, 2), dtype=jnp.float32) / width
        state_pert = (
            patch_states.astype(jnp.float32) - jnp.expand_dims(state_mean, (0, 2))
        ).astype(jnp.bfloat16)
        increment = jnp.einsum(
            "mrjcxl,rxmjk->kcrxl", state_pert, row_transform, preferred_element_type=jnp.float32
        )
        result = state_mean.transpose(1, 0, 2, 3)[None] + increment
        return result.reshape(width, -1, lat_rows, lon_cols).astype(jnp.bfloat16)

    arrived = []
    results = []
    for k in range(PIECES):
        low, high = edges[k], edges[k + 1]
        states = background[:, low:high]
        if k == 1:
            states, recv = lax.optimization_barrier((states, recv))
        elif k == 2:
            states, grams = lax.optimization_barrier((states, grams))
        elif k == 3:
            states, row_transform = lax.optimization_barrier((states, row_transform))
        prepared = states.reshape(
            local_members, high - low, rows_local, regions, lon_cols
        ).transpose(3, 0, 1, 2, 4)
        spread = lax.all_to_all(prepared, "region", split_axis=0, concat_axis=0, tiled=True)
        if k == 0:
            spread, buffer = lax.optimization_barrier((spread, buffer))
            recv = lax.all_to_all(
                buffer, ("member", "region"), split_axis=0, concat_axis=0, tiled=True
            )
            spread, recv = lax.optimization_barrier((spread, recv))
        elif k == 1:
            grams = band_grams(recv, width, lat_rows)
        elif k == 2:
            transform = band_transforms(grams, width)
            row_transform = jnp.repeat(transform, BAND, axis=0).reshape(
                strips_each, rows_local, members, local_members, width
            )
            sources = (lax.axis_index("member") - jnp.arange(members) + members) % members
            row_transform = jnp.take(row_transform, sources, axis=2)
        elif k == 3:
            results = [analyse(piece, row_transform) for piece in arrived[:2]]
            spread, results = lax.optimization_barrier((spread, results))
        arrived.append([])
        for shift in range(members):
            arrived[k].append(scatter_step(spread, shift, strips_each))
    for k in range(2, PIECES):
        results.append(analyse(arrived[k], row_transform))
    return jnp.concatenate(results, axis=1)


def solution(mesh):
    in_specs = (
        P("member", None, "region", None),
        P(("member", "region"), None),
        P(("member", "region")),
        P(("member", "region")),
        P(("member", "region")),
        P(("member", "region"), None),
    )
    out_specs = P(None, None, "member", "region")
    return jax.shard_map(local, mesh=mesh, in_specs=in_specs, out_specs=out_specs, check_vma=False)
```

time: 544 us -> 434 us (0.80)
  the two profiles are of different devices: /device:TPU:2 before, /device:TPU:0 now
where the time goes in v1:
time: 434 us; the launch traced here: 425 us
  waiting for transfers between devices  247 us (57%)
  starting transfers between devices  67.3 us (16%)
  local copies, waits for them, and re-layouts  55.7 us (13%)
  matrix products  20.9 us (5%)
  Pallas kernels  17.8 us (4%)
  other arithmetic  15.4 us (4%)
    ppermute x12, waiting for transfers between devices, scatter_step(): return lax.ppermute(block, 'member', ring)  160 us
    all_to_all x1, waiting for transfers between devices, local(): lax.all_to_all(buffer, ('member', 'region'), split_axis=0, concat_axis=0,...  48.6 us
    ppermute x12, starting transfers between devices, scatter_step(): return lax.ppermute(block, 'member', ring)  44.8 us
    all_to_all x4, waiting for transfers between devices, local(): lax.all_to_all(prepared, 'region', split_axis=0, concat_axis=0, tiled=True)  38.5 us
    all_to_all x4, starting transfers between devices, local(): lax.all_to_all(prepared, 'region', split_axis=0, concat_axis=0, tiled=True)  18.5 us
    reshape x4, local copies, waits for them, and re-layouts, local(): states.reshape(local_members, high - low, rows_local, regions, lon_cols)  12.6 us
    dot_general x12, matrix products, batched(): jnp.einsum('bij,bjk->bik', left, right, precision=lax.Precision.HIGHEST)  11 us
    pallas_call x1, Pallas kernels, band_grams(): pl.pallas_call(functools.partial(gram_kernel, width, lat_rows), grid=(slo...  10.7 us
  transfers between devices with their start and end apart: 17, of which 10 were waited for; matrix products, arithmetic and copies ran while one was open for 16% of the time, Pallas kernels for 2%

profile of v1, /device:TPU:0, one launch (start us, length us, event | category | flops | bytes accessed | tf_op | source)
XLA Modules:
  0.0 425.3 jit_solution(17192574835024121748)
XLA Ops:
  0.0 6.2 %fusion.61 = (bf16[16,3,24,1024]{3,2,1,0:T(8,128)(2,1)S(1)}, bf16[16,3,24,1024]{3,2,1,0:T(8,128)(2,1)}, bf16[16,3,24,1024]{3,2,1,0:T(8,128)(2,1)}) fusion(bf16[16,13,24,1024]{3,2,1,0:T(8,128)(2,1)} %param.6), kind=kLoop, calls=%fused_computation.117 | loop fusion | bytes 14155776 | tf_op jit(solution)/shard_map/slice | solution.py:203
  9.8 5.3 %all-to-all-start = ((bf16[8,16,3,24,128]{4,1,2,3,0:T(8,128)(2,1)}), bf16[8,16,3,24,128]{4,1,2,3,0:T(8,128)(2,1)S(1)}, u32[]{:S(2)}, u32[]{:S(2)}) async-start(bf16[8,16,3,24,128]{4,1,2,3,0:T(8,128)(2,1)} %bitcast.184), calls=%async_computation | async-start | bytes 4718592 | tf_op jit(solution)/shard_map/all_to_all | solution.py:213
  24.2 6.2 %concatenate.6 = bf16[4096,128]{1,0:T(8,128)(2,1)S(1)} concatenate(bf16[4096,64]{1,0:T(8,128)(2,1)} %copy.25, bf16[4096,1]{1,0:T(8,128)(2,1)} %stack.92, bf16[4096,1]{1,0:T(8,128)(2,1)} %stack.93, bf16[4096,1]{1,0:T(8,128)(2,1)} %stack.94, bf16[4096,61]{1,0:T(8,128)(2,1)} %broadcast_in_dim.16), dimensions={1} | concatenate | bytes 2097152 | tf_op jit(solution)/shard_map/concatenate | solution.py:177
  30.6 7.1 %shard_map.64 = bf16[8192,128]{1,0:T(8,128)(2,1)} custom-call(s32[4096]{0:T(1024)S(1)} %add.157.slots_ref, f32[4096,128]{1,0:T(8,128)S(1)} %convert_element_type.86.packed_ref), custom_call_target="tpu_custom_call" | custom-call | flops 4294967296 | bytes 4194304 | tf_op jit(solution)/shard_map/pallas_call | solution.py:138
  37.7 6.8 %all-to-all-done = bf16[8,16,3,24,128]{4,1,2,3,0:T(8,128)(2,1)S(1)} async-done(((bf16[8,16,3,24,128]{4,1,2,3,0:T(8,128)(2,1)}), bf16[8,16,3,24,128]{4,1,2,3,0:T(8,128)(2,1)S(1)}, u32[]{:S(2)}, u32[]{:S(2)}) %all-to-all-start) | async-done | bytes 2359328 | tf_op jit(solution)/shard_map/all_to_all | solution.py:213
  46.0 4.0 all-to-all-start.1
  50.1 48.6 %all-to-all-done.1 = bf16[32,256,128]{2,1,0:T(8,128)(2,1)S(1)} async-done(((bf16[32,256,128]{2,1,0:T(8,128)(2,1)}), bf16[32,256,128]{2,1,0:T(8,128)(2,1)S(1)}, u32[]{:S(2)}, u32[]{:S(2)}) %all-to-all-start.1) | async-done | bytes 2097184 | tf_op jit(solution)/shard_map/all_to_all | solution.py:216
  98.7 10.7 %shard_map.65 = (f32[1536,64]{1,0:T(8,128)S(1)}, f32[24,64]{1,0:T(8,128)S(1)}) custom-call(bf16[8192,128]{1,0:T(8,128)(2,1)S(1)} %bitcast.173), custom_call_target="tpu_custom_call" | custom-call | flops 6442450944 | bytes 2097152 | tf_op jit(solution)/shard_map/pallas_call | solution.py:60
  113.0 5.0 %all-to-all-start.4 = ((bf16[8,16,3,24,128]{4,1,2,3,0:T(8,128)(2,1)}), bf16[8,16,3,24,128]{4,1,2,3,0:T(8,128)(2,1)}, u32[]{:S(2)}, u32[]{:S(2)}) async-start(bf16[8,16,3,24,128]{4,1,2,3,0:T(8,128)(2,1)} %bitcast.185), calls=%async_computation.4 | async-start | bytes 4718592 | tf_op jit(solution)/shard_map/all_to_all | solution.py:213
  128.4 19.1 %all-to-all-done.4 = bf16[8,16,3,24,128]{4,1,2,3,0:T(8,128)(2,1)} async-done(((bf16[8,16,3,24,128]{4,1,2,3,0:T(8,128)(2,1)}), bf16[8,16,3,24,128]{4,1,2,3,0:T(8,128)(2,1)}, u32[]{:S(2)}, u32[]{:S(2)}) %all-to-all-start.4) | async-done | bytes 2359328 | tf_op jit(solution)/shard_map/all_to_all | solution.py:213
  147.5 4.5 %all-to-all-start.3 = ((bf16[8,16,3,24,128]{4,1,2,3,0:T(8,128)(2,1)}), bf16[8,16,3,24,128]{4,1,2,3,0:T(8,128)(2,1)}, u32[]{:S(2)}, u32[]{:S(2)}) async-start(bf16[8,16,3,24,128]{4,1,2,3,0:T(8,128)(2,1)} %bitcast.171), calls=%async_computation.3 | async-start | bytes 4718592 | tf_op jit(solution)/shard_map/all_to_all | solution.py:213
  165.2 3.7 copy.83
  168.9 12.6 %all-to-all-done.3 = bf16[8,16,3,24,128]{4,1,2,3,0:T(8,128)(2,1)} async-done(((bf16[8,16,3,24,128]{4,1,2,3,0:T(8,128)(2,1)}), bf16[8,16,3,24,128]{4,1,2,3,0:T(8,128)(2,1)}, u32[]{:S(2)}, u32[]{:S(2)}) %all-to-all-start.3) | async-done | bytes 2359328 | tf_op jit(solution)/shard_map/all_to_all | solution.py:213
  181.5 3.7 all-to-all-start.2
  189.8 14.3 %collective-permute-done.2 = bf16[2,16,3,24,128]{4,1,2,3,0:T(8,128)(2,1)S(1)} collective-permute-done((bf16[2,16,3,24,128]{4,1,2,3,0:T(8,128)(2,1)S(1)}, bf16[2,16,3,24,128]{4,1,2,3,0:T(8,128)(2,1)S(1)}, u32[]{:S(2)}, u32[]{:S(2)}) %collective-permute-start.2) | collective-permute-done | bytes 589856 | tf_op jit(solution)/shard_map/ppermute | solution.py:161
  204.1 35.7 %collective-permute-done.1 = bf16[2,16,3,24,128]{4,1,2,3,0:T(8,128)(2,1)S(1)} collective-permute-done((bf16[2,16,3,24,128]{4,1,2,3,0:T(8,128)(2,1)S(1)}, bf16[2,16,3,24,128]{4,1,2,3,0:T(8,128)(2,1)S(1)}, u32[]{:S(2)}, u32[]{:S(2)}) %collective-permute-start.1) | collective-permute-done | bytes 589856 | tf_op jit(solution)/shard_map/ppermute | solution.py:161
  250.5 3.2 dynamic-slice_bitcast_fusion.1
  255.6 4.5 %collective-permute-done.5 = bf16[2,16,3,24,128]{4,1,2,3,0:T(8,128)(2,1)S(1)} collective-permute-done((bf16[2,16,3,24,128]{4,1,2,3,0:T(8,128)(2,1)S(1)}, bf16[2,16,3,24,128]{4,1,2,3,0:T(8,128)(2,1)S(1)}, u32[]{:S(2)}, u32[]{:S(2)}) %collective-permute-start.5) | collective-permute-done | bytes 589856 | tf_op jit(solution)/shard_map/ppermute | solution.py:161
  262.3 37.3 %collective-permute-done.4 = bf16[2,16,3,24,128]{4,1,2,3,0:T(8,128)(2,1)S(1)} collective-permute-done((bf16[2,16,3,24,128]{4,1,2,3,0:T(8,128)(2,1)S(1)}, bf16[2,16,3,24,128]{4,1,2,3,0:T(8,128)(2,1)S(1)}, u32[]{:S(2)}, u32[]{:S(2)}) %collective-permute-start.4) | collective-permute-done | bytes 589856 | tf_op jit(solution)/shard_map/ppermute | solution.py:161
  304.0 24.1 %collective-permute-start.10 = (bf16[2,16,4,24,128]{4,1,2,3,0:T(8,128)(2,1)S(1)}, bf16[2,16,4,24,128]{4,1,2,3,0:T(8,128)(2,1)S(1)}, u32[]{:S(2)}, u32[]{:S(2)}) collective-permute-start(bf16[2,16,4,24,128]{4,1,2,3,0:T(8,128)(2,1)S(1)} %get-tuple-element.42), channel_id=1, source_target_pairs={{0,16},{8,24},{16,0},{24,8},{1,17},{9,25},{17,1},{25,9},{2,18},{10... | collective-permute-start | bytes 2359304 | tf_op jit(solution)/shard_map/ppermute | solution.py:161
  328.0 8.8 %collective-permute-start.9 = (bf16[2,16,4,24,128]{4,1,2,3,0:T(8,128)(2,1)S(1)}, bf16[2,16,4,24,128]{4,1,2,3,0:T(8,128)(2,1)S(1)}, u32[]{:S(2)}, u32[]{:S(2)}) collective-permute-start(bf16[2,16,4,24,128]{4,1,2,3,0:T(8,128)(2,1)S(1)} %get-tuple-element.43), channel_id=1, source_target_pairs={{0,8},{8,16},{16,24},{24,0},{1,9},{9,17},{17,25},{25,1},{2,10},{10... | collective-permute-start | bytes 2359304 | tf_op jit(solution)/shard_map/ppermute | solution.py:161
  336.8 45.8 %collective-permute-done.7 = bf16[2,16,3,24,128]{4,1,2,3,0:T(8,128)(2,1)} collective-permute-done((bf16[2,16,3,24,128]{4,1,2,3,0:T(8,128)(2,1)}, bf16[2,16,3,24,128]{4,1,2,3,0:T(8,128)(2,1)}, u32[]{:S(2)}, u32[]{:S(2)}) %collective-permute-start.7) | collective-permute-done | bytes 589856 | tf_op jit(solution)/shard_map/ppermute | solution.py:161
  392.6 22.4 %collective-permute-done.10 = bf16[2,16,4,24,128]{4,1,2,3,0:T(8,128)(2,1)S(1)} collective-permute-done((bf16[2,16,4,24,128]{4,1,2,3,0:T(8,128)(2,1)S(1)}, bf16[2,16,4,24,128]{4,1,2,3,0:T(8,128)(2,1)S(1)}, u32[]{:S(2)}, u32[]{:S(2)}) %collective-permute-start.10) | collective-permute-done | bytes 786464 | tf_op jit(solution)/shard_map/ppermute | solution.py:161
  420.1 4.8 %pad_maximum_fusion = bf16[64,13,48,128]{3,2,1,0:T(8,128)(2,1)} fusion(bf16[64,4,48,128]{3,2,1,0:T(8,128)(2,1)S(1)} %copy.47, bf16[64,3,48,128]{3,2,1,0:T(8,128)(2,1)S(1)} %copy.46, bf16[64,3,48,128]{3,2,1,0:T(8,128)(2,1)S(1)} %copy.45, bf16[64,3,48,128]{3,2,1,0:T(8,128)(2,1)S(1)} %copy.44), kind=kLoop, calls=%fused_computation.1 | loop fusion | flops 15335424 | bytes 20447232 | tf_op jit(solution)/shard_map/concatenate | solution.py:237
  (112 shorter events, 79.8 us)
Async XLA Ops:
  9.8 8.8 %copy-start.8 = (bf16[4096,64]{0,1:T(8,128)(2,1)S(1)}, bf16[4096,64]{0,1:T(8,128)(2,1)}, u32[]{:S(2)}) copy-start(bf16[4096,64]{0,1:T(8,128)(2,1)} %param.7) | copy-start | bytes 1572868
  9.8 34.8 %all-to-all-start = ((bf16[8,16,3,24,128]{4,1,2,3,0:T(8,128)(2,1)}), bf16[8,16,3,24,128]{4,1,2,3,0:T(8,128)(2,1)S(1)}, u32[]{:S(2)}, u32[]{:S(2)}) async-start(bf16[8,16,3,24,128]{4,1,2,3,0:T(8,128)(2,1)} %bitcast.184), calls=%async_computation | async-start | bytes 4718592 | tf_op jit(solution)/shard_map/all_to_all | solution.py:213
  15.2 6.4 %copy-start.12 = (bf16[4096]{0:T(1024)(128)(2,1)S(1)}, bf16[4096]{0:T(1024)(128)(2,1)}, u32[]{:S(2)}) copy-start(bf16[4096]{0:T(1024)(128)(2,1)} %param.9) | copy-start | bytes 24580
  46.0 52.7 %all-to-all-start.1 = ((bf16[32,256,128]{2,1,0:T(8,128)(2,1)}), bf16[32,256,128]{2,1,0:T(8,128)(2,1)S(1)}, u32[]{:S(2)}, u32[]{:S(2)}) async-start(bf16[32,256,128]{2,1,0:T(8,128)(2,1)} %bitcast.4), calls=%async_computation.1 | async-start | bytes 4194304 | tf_op jit(solution)/shard_map/all_to_all | solution.py:216
  98.7 10.7 %copy-start.1 = (bf16[16,3,24,1024]{3,2,1,0:T(8,128)(2,1)S(1)}, bf16[16,3,24,1024]{3,2,1,0:T(8,128)(2,1)}, u32[]{:S(2)}) copy-start(bf16[16,3,24,1024]{3,2,1,0:T(8,128)(2,1)} %get-tuple-element.35) | copy-start | bytes 7077892
  113.0 34.4 %all-to-all-start.4 = ((bf16[8,16,3,24,128]{4,1,2,3,0:T(8,128)(2,1)}), bf16[8,16,3,24,128]{4,1,2,3,0:T(8,128)(2,1)}, u32[]{:S(2)}, u32[]{:S(2)}) async-start(bf16[8,16,3,24,128]{4,1,2,3,0:T(8,128)(2,1)} %bitcast.185), calls=%async_computation.4 | async-start | bytes 4718592 | tf_op jit(solution)/shard_map/all_to_all | solution.py:213
  147.5 34.0 %all-to-all-start.3 = ((bf16[8,16,3,24,128]{4,1,2,3,0:T(8,128)(2,1)}), bf16[8,16,3,24,128]{4,1,2,3,0:T(8,128)(2,1)}, u32[]{:S(2)}, u32[]{:S(2)}) async-start(bf16[8,16,3,24,128]{4,1,2,3,0:T(8,128)(2,1)} %bitcast.171), calls=%async_computation.3 | async-start | bytes 4718592 | tf_op jit(solution)/shard_map/all_to_all | solution.py:213
  156.7 7.6 %slice-start = ((bf16[16,13,24,1024]{3,2,1,0:T(8,128)(2,1)}), bf16[16,4,24,1024]{3,2,1,0:T(8,128)(2,1)S(1)}, s32[]{:S(2)}) async-start(bf16[16,13,24,1024]{3,2,1,0:T(8,128)(2,1)} %param.6), calls=%async_computation.5 | async-start | bytes 6291456 | tf_op jit(solution)/shard_map/slice | solution.py:203
  181.5 121.6 %all-to-all-start.2 = ((bf16[8,16,4,24,128]{4,1,2,3,0:T(8,128)(2,1)}), bf16[8,16,4,24,128]{4,1,2,3,0:T(8,128)(2,1)S(1)}, u32[]{:S(2)}, u32[]{:S(2)}) async-start(bf16[8,16,4,24,128]{4,1,2,3,0:T(8,128)(2,1)} %bitcast.178), calls=%async_computation.2 | async-start | bytes 6291456 | tf_op jit(solution)/shard_map/all_to_all | solution.py:213
  187.2 16.9 %collective-permute-start.2 = (bf16[2,16,3,24,128]{4,1,2,3,0:T(8,128)(2,1)S(1)}, bf16[2,16,3,24,128]{4,1,2,3,0:T(8,128)(2,1)S(1)}, u32[]{:S(2)}, u32[]{:S(2)}) collective-permute-start(bf16[2,16,3,24,128]{4,1,2,3,0:T(8,128)(2,1)S(1)} %get-tuple-element.53), channel_id=1, source_target_pairs={{0,24},{8,0},{16,8},{24,16},{1,25},{9,1},{17,9},{25,17},{2,26},{10... | collective-permute-start | bytes 1769480 | tf_op jit(solution)/shard_map/ppermute | solution.py:161
  189.1 50.7 %collective-permute-start.1 = (bf16[2,16,3,24,128]{4,1,2,3,0:T(8,128)(2,1)S(1)}, bf16[2,16,3,24,128]{4,1,2,3,0:T(8,128)(2,1)S(1)}, u32[]{:S(2)}, u32[]{:S(2)}) collective-permute-start(bf16[2,16,3,24,128]{4,1,2,3,0:T(8,128)(2,1)S(1)} %get-tuple-element.54), channel_id=1, source_target_pairs={{0,16},{8,24},{16,0},{24,8},{1,17},{9,25},{17,1},{25,9},{2,18},{10... | collective-permute-start | bytes 1769480 | tf_op jit(solution)/shard_map/ppermute | solution.py:161
  189.1 50.7 %collective-permute-start = (bf16[2,16,3,24,128]{4,1,2,3,0:T(8,128)(2,1)S(1)}, bf16[2,16,3,24,128]{4,1,2,3,0:T(8,128)(2,1)S(1)}, u32[]{:S(2)}, u32[]{:S(2)}) collective-permute-start(bf16[2,16,3,24,128]{4,1,2,3,0:T(8,128)(2,1)S(1)} %get-tuple-element.55), channel_id=1, source_target_pairs={{0,8},{8,16},{16,24},{24,0},{1,9},{9,17},{17,25},{25,1},{2,10},{10... | collective-permute-start | bytes 1769480 | tf_op jit(solution)/shard_map/ppermute | solution.py:161
  239.8 8.6 %copy-start.6 = (bf16[2,24,4,16,64]{4,3,1,0,2:T(8,128)(2,1)S(1)}, bf16[2,24,4,16,64]{4,3,1,0,2:T(8,128)(2,1)}, u32[]{:S(2)}) copy-start(bf16[2,24,4,16,64]{4,3,1,0,2:T(8,128)(2,1)} %select_bitcast_fusion) | copy-start | bytes 1179652
  243.1 17.0 %collective-permute-start.5 = (bf16[2,16,3,24,128]{4,1,2,3,0:T(8,128)(2,1)S(1)}, bf16[2,16,3,24,128]{4,1,2,3,0:T(8,128)(2,1)S(1)}, u32[]{:S(2)}, u32[]{:S(2)}) collective-permute-start(bf16[2,16,3,24,128]{4,1,2,3,0:T(8,128)(2,1)S(1)} %get-tuple-element.49), channel_id=1, source_target_pairs={{0,24},{8,0},{16,8},{24,16},{1,25},{9,1},{17,9},{25,17},{2,26},{10... | collective-permute-start | bytes 1769480 | tf_op jit(solution)/shard_map/ppermute | solution.py:161
  243.2 56.5 %collective-permute-start.4 = (bf16[2,16,3,24,128]{4,1,2,3,0:T(8,128)(2,1)S(1)}, bf16[2,16,3,24,128]{4,1,2,3,0:T(8,128)(2,1)S(1)}, u32[]{:S(2)}, u32[]{:S(2)}) collective-permute-start(bf16[2,16,3,24,128]{4,1,2,3,0:T(8,128)(2,1)S(1)} %get-tuple-element.50), channel_id=1, source_target_pairs={{0,16},{8,24},{16,0},{24,8},{1,17},{9,25},{17,1},{25,9},{2,18},{10... | collective-permute-start | bytes 1769480 | tf_op jit(solution)/shard_map/ppermute | solution.py:161
  246.2 53.4 %collective-permute-start.3 = (bf16[2,16,3,24,128]{4,1,2,3,0:T(8,128)(2,1)S(1)}, bf16[2,16,3,24,128]{4,1,2,3,0:T(8,128)(2,1)S(1)}, u32[]{:S(2)}, u32[]{:S(2)}) collective-permute-start(bf16[2,16,3,24,128]{4,1,2,3,0:T(8,128)(2,1)S(1)} %get-tuple-element.51), channel_id=1, source_target_pairs={{0,8},{8,16},{16,24},{24,0},{1,9},{9,17},{17,25},{25,1},{2,10},{10... | collective-permute-start | bytes 1769480 | tf_op jit(solution)/shard_map/ppermute | solution.py:161
  253.7 74.3 %collective-permute-start.8 = (bf16[2,16,3,24,128]{4,1,2,3,0:T(8,128)(2,1)}, bf16[2,16,3,24,128]{4,1,2,3,0:T(8,128)(2,1)}, u32[]{:S(2)}, u32[]{:S(2)}) collective-permute-start(bf16[2,16,3,24,128]{4,1,2,3,0:T(8,128)(2,1)} %get-tuple-element.45), channel_id=1, source_target_pairs={{0,24},{8,0},{16,8},{24,16},{1,25},{9,1},{17,9},{25,17},{2,26},{10... | collective-permute-start | bytes 1769480 | tf_op jit(solution)/shard_map/ppermute | solution.py:161
  255.6 127.0 %collective-permute-start.7 = (bf16[2,16,3,24,128]{4,1,2,3,0:T(8,128)(2,1)}, bf16[2,16,3,24,128]{4,1,2,3,0:T(8,128)(2,1)}, u32[]{:S(2)}, u32[]{:S(2)}) collective-permute-start(bf16[2,16,3,24,128]{4,1,2,3,0:T(8,128)(2,1)} %get-tuple-element.46), channel_id=1, source_target_pairs={{0,16},{8,24},{16,0},{24,8},{1,17},{9,25},{17,1},{25,9},{2,18},{10... | collective-permute-start | bytes 1769480 | tf_op jit(solution)/shard_map/ppermute | solution.py:161
  260.1 122.5 %collective-permute-start.6 = (bf16[2,16,3,24,128]{4,1,2,3,0:T(8,128)(2,1)}, bf16[2,16,3,24,128]{4,1,2,3,0:T(8,128)(2,1)}, u32[]{:S(2)}, u32[]{:S(2)}) collective-permute-start(bf16[2,16,3,24,128]{4,1,2,3,0:T(8,128)(2,1)} %get-tuple-element.47), channel_id=1, source_target_pairs={{0,8},{8,16},{16,24},{24,0},{1,9},{9,17},{17,25},{25,1},{2,10},{10... | collective-permute-start | bytes 1769480 | tf_op jit(solution)/shard_map/ppermute | solution.py:161
  303.1 79.5 %copy-start.5 = (bf16[1,2,16,3,24,128]{5,2,0,3,4,1:T(8,128)(2,1)S(1)}, bf16[1,2,16,3,24,128]{5,2,0,3,4,1:T(8,128)(2,1)}, u32[]{:S(2)}) copy-start(bf16[1,2,16,3,24,128]{5,2,0,3,4,1:T(8,128)(2,1)} %get-tuple-element.44) | copy-start | bytes 1769476
  303.1 82.3 %copy-start.7 = (bf16[2,24,4,16,64]{4,3,1,0,2:T(8,128)(2,1)S(1)}, bf16[2,24,4,16,64]{4,3,1,0,2:T(8,128)(2,1)}, u32[]{:S(2)}) copy-start(bf16[2,24,4,16,64]{4,3,1,0,2:T(8,128)(2,1)} %select_bitcast_fusion) | copy-start | bytes 1179652
  303.9 88.7 %collective-permute-start.11 = (bf16[2,16,4,24,128]{4,1,2,3,0:T(8,128)(2,1)S(1)}, bf16[2,16,4,24,128]{4,1,2,3,0:T(8,128)(2,1)S(1)}, u32[]{:S(2)}, u32[]{:S(2)}) collective-permute-start(bf16[2,16,4,24,128]{4,1,2,3,0:T(8,128)(2,1)S(1)} %get-tuple-element.41), channel_id=1, source_target_pairs={{0,24},{8,0},{16,8},{24,16},{1,25},{9,1},{17,9},{25,17},{2,26},{10... | collective-permute-start | bytes 2359304 | tf_op jit(solution)/shard_map/ppermute | solution.py:161
  304.0 111.1 %collective-permute-start.10 = (bf16[2,16,4,24,128]{4,1,2,3,0:T(8,128)(2,1)S(1)}, bf16[2,16,4,24,128]{4,1,2,3,0:T(8,128)(2,1)S(1)}, u32[]{:S(2)}, u32[]{:S(2)}) collective-permute-start(bf16[2,16,4,24,128]{4,1,2,3,0:T(8,128)(2,1)S(1)} %get-tuple-element.42), channel_id=1, source_target_pairs={{0,16},{8,24},{16,0},{24,8},{1,17},{9,25},{17,1},{25,9},{2,18},{10... | collective-permute-start | bytes 2359304 | tf_op jit(solution)/shard_map/ppermute | solution.py:161
  328.0 87.0 %collective-permute-start.9 = (bf16[2,16,4,24,128]{4,1,2,3,0:T(8,128)(2,1)S(1)}, bf16[2,16,4,24,128]{4,1,2,3,0:T(8,128)(2,1)S(1)}, u32[]{:S(2)}, u32[]{:S(2)}) collective-permute-start(bf16[2,16,4,24,128]{4,1,2,3,0:T(8,128)(2,1)S(1)} %get-tuple-element.43), channel_id=1, source_target_pairs={{0,8},{8,16},{16,24},{24,0},{1,9},{9,17},{17,25},{25,1},{2,10},{10... | collective-permute-start | bytes 2359304 | tf_op jit(solution)/shard_map/ppermute | solution.py:161
  (7 other events, 26.1 us)
